TPU v7x, 512 devices: a whole 4x8x8 slice. The times are simulated.
512 devices in a mesh: seq: 128 (over y, z, core), head: 4 (over x).
Axes of the slice: x: 4, y: 8, z: 8, core: 2. Of those that a mesh axis runs over, the one named last changes fastest.
Arguments:
- queries: bfloat16 [16384, 4096], P('seq', 'head'), may hold values from -6 to 6
- keys: bfloat16 [16384, 4096], P('seq', 'head'), may hold values from -6 to 6
- values: bfloat16 [16384, 4096], P('seq', 'head'), may hold values from -6 to 6
- hidden: bfloat16 [16384, 2048], P('seq', 'head'), may hold values from -6 to 6
- gate_weight: bfloat16 [2048, 256], P('head'), may hold values from -0.125 to 0.125
- level_slot: int32 [8], replicated, may hold values from 0 to 7, each once
- out_grad: bfloat16 [16384, 4096], P('seq', 'head'), may hold values from -6 to 6
Outputs:
- mixed: bfloat16 [16384, 4096], P('seq', 'head')
- grad_queries: bfloat16 [16384, 4096], P('seq', 'head')
- grad_keys: bfloat16 [16384, 4096], P('seq', 'head')
- grad_values: bfloat16 [16384, 4096], P('seq', 'head')
- grad_hidden: bfloat16 [16384, 2048], P('seq', 'head')
Inputs may be any that keep to these rules, and one draw needn't show every extreme that they name: `level_slot`: each column index of a head's block appears once.
All inputs are finite; a program needn't handle non-finite values.
Results may differ from a plain program's by a relative error of at most 0.01.
Values may be sent and summed in bfloat16 or wider, within the bound.
No kernel may reach another device: no remote copies, remote signals or barrier semaphores. Data moves between devices by JAX's collectives and lax.ppermute only.
A program may use at most 64 MiB of HBM per device.

v0:
```python
import jax
import jax.numpy as jnp
from jax import lax
from jax.sharding import PartitionSpec as P

DK = 128
SPAN = 128
HIGH = lax.Precision.HIGHEST


def from_partner(block, axis, stride):
    count = lax.axis_size(axis)
    route = []
    for low in range(count):
        high = low | 1 << stride
        if high != low and high < count:
            route += [(low, high), (high, low)]
    return lax.ppermute(block, axis, route)


def local(queries, keys, values, hidden, gate_weight, level_slot, out_grad):
    tok_rows = queries.shape[0]
    heads_here = queries.shape[1] // DK
    levels = level_slot.shape[0]
    rows_here = heads_here * levels
    span_count = tok_rows // SPAN
    local_bits = span_count.bit_length() - 1
    device_bits = lax.axis_size("seq").bit_length() - 1
    seq_index = lax.axis_index("seq")
    weight_cols = lax.all_to_all(gate_weight, "head", split_axis=1, concat_axis=0, tiled=True)
    logits = lax.dot_general(
        weight_cols,
        lax.all_gather(hidden, "head", axis=1, tiled=True),
        (((0,), (1,)), ((), ())),
        preferred_element_type=jnp.float32,
    )
    slot_table = (level_slot[:, None] == jnp.arange(levels, dtype=jnp.int32)[None, :]).astype(
        jnp.float32
    )
    chosen = jnp.einsum(
        "lm,hmt->hlt", slot_table, logits.reshape(heads_here, levels, tok_rows), precision=HIGH
    )
    weights = jnp.transpose(jax.nn.softplus(chosen), (2, 0, 1))
    query_heads = queries.reshape(tok_rows, heads_here, DK)
    grad_heads = out_grad.reshape(tok_rows, heads_here, DK)
    query_blocks = queries.reshape(span_count, SPAN, heads_here, DK)
    key_blocks = keys.reshape(span_count, SPAN, heads_here, DK)
    value_blocks = values.reshape(span_count, SPAN, heads_here, DK)
    position = jnp.arange(SPAN)
    causal = (position[:, None] >= position[None, :]).astype(jnp.float32)
    scores = jnp.einsum(
        "nchd,nshd->nhcs", query_blocks, key_blocks, preferred_element_type=jnp.float32
    )
    attend = (scores * causal / SPAN).astype(jnp.bfloat16)
    intra = jnp.einsum(
        "nhcs,nshe->nche", attend, value_blocks, preferred_element_type=jnp.float32
    ).reshape(tok_rows, heads_here, DK)
    weighted = (weights[..., None] * grad_heads[:, :, None, :]).astype(jnp.bfloat16)
    device_grads = jnp.einsum(
        "thd,thje->hjde",
        query_heads,
        weighted[:, :, 1 + local_bits :],
        preferred_element_type=jnp.float32,
    )
    span_states = jnp.einsum(
        "nchd,nche->nhde", key_blocks, value_blocks, preferred_element_type=jnp.float32
    )
    device_state = span_states.sum(0)
    group = device_state
    lower_states = []
    for bit_pos in range(device_bits):
        partner = from_partner(group.astype(jnp.bfloat16), "seq", bit_pos).astype(group.dtype)
        upper_half = seq_index >> bit_pos & 1
        lower_states.append(
            jnp.where(upper_half == 1, partner, 0.0) / float((1 << bit_pos) * tok_rows)
        )
        group = group + partner
    pending = device_grads
    carried = jnp.zeros_like(device_state)
    for bit_pos in range(device_bits):
        partner_pending = from_partner(pending.astype(jnp.bfloat16), "seq", bit_pos).astype(
            pending.dtype
        )
        upper_half = seq_index >> bit_pos & 1
        scale_here = float((1 << bit_pos) * tok_rows)
        carried = carried + jnp.where(upper_half == 0, partner_pending[:, 0], 0.0) / scale_here
        pending = pending[:, 1:] + partner_pending[:, 1:]
    device_level = jnp.stack(lower_states, 1).astype(jnp.bfloat16)
    device_outs = jnp.einsum(
        "thd,hjde->tjhe", query_heads, device_level, preferred_element_type=jnp.float32
    )
    mixed = weights[:, :, 0:1] * intra + jnp.einsum(
        "thj,tjhe->the", weights[:, :, 1:], device_outs, precision=HIGH
    )
    first_grad = jnp.sum(grad_heads * intra, -1)
    later_grad = jnp.einsum(
        "the,tjhe->thj", grad_heads.astype(jnp.float32), device_outs, precision=HIGH
    )
    weight_grad = jnp.concatenate([first_grad[:, :, None], later_grad], 2)
    first_blocks = weighted[:, :, 0].reshape(span_count, SPAN, heads_here, DK)
    grad_score = (
        jnp.einsum(
            "nche,nshe->nhcs", first_blocks, value_blocks, preferred_element_type=jnp.float32
        )
        * causal
        / SPAN
    ).astype(jnp.bfloat16)
    grad_query = jnp.einsum(
        "nhcs,nshd->nchd", grad_score, key_blocks, preferred_element_type=jnp.float32
    ).reshape(tok_rows, heads_here, DK)
    grad_key = jnp.einsum(
        "nhcs,nchd->nshd", grad_score, query_blocks, preferred_element_type=jnp.float32
    ).reshape(tok_rows, heads_here, DK)
    grad_value = jnp.einsum(
        "nhcs,nche->nshe", attend, first_blocks, preferred_element_type=jnp.float32
    ).reshape(tok_rows, heads_here, DK)
    device_back = jnp.einsum(
        "the,hjde->tjhd", grad_heads, device_level, preferred_element_type=jnp.float32
    )
    grad_query = grad_query + jnp.einsum(
        "thj,tjhd->thd", weights[:, :, 1 + local_bits :], device_back, precision=HIGH
    )
    state_total = carried[None].astype(jnp.bfloat16)
    grad_key = grad_key + jnp.einsum(
        "nche,nhde->nchd", value_blocks, state_total, preferred_element_type=jnp.float32
    ).reshape(tok_rows, heads_here, DK)
    grad_value = grad_value + jnp.einsum(
        "nchd,nhde->nche", key_blocks, state_total, preferred_element_type=jnp.float32
    ).reshape(tok_rows, heads_here, DK)
    chosen_grad = jnp.transpose(weight_grad, (1, 2, 0)) * jax.nn.sigmoid(chosen)
    logit_grad = (
        jnp.einsum("lm,hlt->hmt", slot_table, chosen_grad, precision=HIGH)
        .reshape(rows_here, tok_rows)
        .astype(jnp.bfloat16)
    )
    partial_grad = lax.dot_general(
        logit_grad, weight_cols, (((0,), (1,)), ((), ())), preferred_element_type=jnp.float32
    )
    grad_hidden = lax.psum_scatter(partial_grad, "head", scatter_dimension=1, tiled=True)
    width_all = heads_here * DK
    return (
        mixed.reshape(tok_rows, width_all).astype(jnp.bfloat16),
        grad_query.reshape(tok_rows, width_all).astype(jnp.bfloat16),
        grad_key.reshape(tok_rows, width_all).astype(jnp.bfloat16),
        grad_value.reshape(tok_rows, width_all).astype(jnp.bfloat16),
        grad_hidden.astype(jnp.bfloat16),
    )


def solution(mesh):
    placed = (
        P("seq", "head"),
        P("seq", "head"),
        P("seq", "head"),
        P("seq", "head"),
        P("head", None),
        P(),
        P("seq", "head"),
    )
    return jax.shard_map(
        local,
        mesh=mesh,
        in_specs=placed,
        out_specs=(
            P("seq", "head"),
            P("seq", "head"),
            P("seq", "head"),
            P("seq", "head"),
            P("seq", "head"),
        ),
        check_vma=False,
    )
```

profile of v0, /device:TPU:1, one launch (start us, length us, event | category | flops | bytes accessed | tf_op | source)
XLA Modules:
  0.0 322.8 jit_solution(2008449599605130262)
XLA Ops:
  7.2 1.9 copy.36
  9.1 4.8 %all-to-all-start = ((bf16[512,4,64]{0,2,1:T(8,128)(2,1)}), bf16[512,4,64]{0,2,1:T(8,128)(2,1)S(1)}, u32[]{:S(2)}, u32[]{:S(2)}) async-start(bf16[512,4,64]{0,2,1:T(8,128)(2,1)} %bitcast.3), calls=%async_computation | async-start | bytes 524288 | tf_op jit(solution)/shard_map/all_to_all | solution.py:30
  13.9 1.1 copy.47
  15.0 1.1 copy.101
  16.4 12.0 %all_gather.3 = bf16[128,2048]{1,0:T(8,128)(2,1)S(1)} all-gather(bf16[128,512]{1,0:T(8,128)(2,1)S(1)} %copy-done.34), channel_id=1, replica_groups=mesh['seq'=128,'head'=4] {'head'}, dimensions={1}, use_global_device_ids=true | all-gather | bytes 655360 | tf_op jit(solution)/shard_map/all_gather | solution.py:33
  29.0 1.3 multiply_convert_fusion
  30.3 3.2 fusion.114
  33.5 9.3 %collective-permute-start.7 = (bf16[8,7,128,128]{2,3,1,0:T(8,128)(2,1)}, bf16[8,7,128,128]{2,3,1,0:T(8,128)(2,1)}, u32[]{:S(2)}, u32[]{:S(2)}) collective-permute-start(bf16[8,7,128,128]{2,3,1,0:T(8,128)(2,1)} %get-tuple-element.35), channel_id=1, source_target_pairs={{0,4},{4,0},{8,12},{12,8},{16,20},{20,16},{24,28},{28,24},{32,36},... | collective-permute-start | bytes 5505032 | tf_op jit(solution)/shard_map/ppermute | solution.py:18
  43.8 1.9 collective-permute-start
  45.7 1.5 collective-permute-done
  47.3 2.2 collective-permute-start.1
  49.5 1.9 convert_element_type.195
  51.5 3.3 %fusion.111 = (bf16[8,6,128,128]{2,3,1,0:T(8,128)(2,1)}, f32[8,6,128,128]{2,3,1,0:T(8,128)}) fusion(f32[8,7,128,128]{2,3,1,0:T(8,128)S(1)} %convert_element_type.195, f32[8,7,128,128]{2,3,1,0:T(8,128)S(1)} %copy-done.2), kind=kLoop, calls=%fused_computation.155 | loop fusion | flops 1572864 | bytes 11010048 | tf_op jit(solution)/shard_map/convert_element_type | solution.py:81
  54.7 3.4 %collective-permute-start.8 = (bf16[8,6,128,128]{2,3,1,0:T(8,128)(2,1)}, bf16[8,6,128,128]{2,3,1,0:T(8,128)(2,1)}, u32[]{:S(2)}, u32[]{:S(2)}) collective-permute-start(bf16[8,6,128,128]{2,3,1,0:T(8,128)(2,1)} %get-tuple-element.23), channel_id=1, source_target_pairs={{0,8},{8,0},{4,12},{12,4},{16,24},{24,16},{20,28},{28,20},{32,40},... | collective-permute-start | bytes 4718600 | tf_op jit(solution)/shard_map/ppermute | solution.py:18
  58.2 1.9 collective-permute-start.2
  60.8 36.5 %collective-permute-done.2 = bf16[8,128,128]{2,1,0:T(8,128)(2,1)S(1)} collective-permute-done((bf16[8,128,128]{2,1,0:T(8,128)(2,1)S(1)}, bf16[8,128,128]{2,1,0:T(8,128)(2,1)S(1)}, u32[]{:S(2)}, u32[]{:S(2)}) %collective-permute-start.2) | collective-permute-done | bytes 262176 | tf_op jit(solution)/shard_map/ppermute | solution.py:18
  97.4 5.9 %collective-permute-start.3 = (bf16[8,128,128]{2,1,0:T(8,128)(2,1)S(1)}, bf16[8,128,128]{2,1,0:T(8,128)(2,1)S(1)}, u32[]{:S(2)}, u32[]{:S(2)}) collective-permute-start(bf16[8,128,128]{2,1,0:T(8,128)(2,1)S(1)} %fusion.47), channel_id=1, source_target_pairs={{0,32},{32,0},{4,36},{36,4},{8,40},{40,8},{12,44},{44,12},{16,48},... | collective-permute-start | bytes 786440 | tf_op jit(solution)/shard_map/ppermute | solution.py:18
  103.5 6.3 %collective-permute-done.3 = bf16[8,128,128]{2,1,0:T(8,128)(2,1)S(1)} collective-permute-done((bf16[8,128,128]{2,1,0:T(8,128)(2,1)S(1)}, bf16[8,128,128]{2,1,0:T(8,128)(2,1)S(1)}, u32[]{:S(2)}, u32[]{:S(2)}) %collective-permute-start.3) | collective-permute-done | bytes 262176 | tf_op jit(solution)/shard_map/ppermute | solution.py:18
  110.0 2.4 collective-permute-start.4
  112.4 1.8 convert_element_type.197
  114.7 11.1 %collective-permute-start.9 = (bf16[8,5,128,128]{2,3,1,0:T(8,128)(2,1)S(1)}, bf16[8,5,128,128]{2,3,1,0:T(8,128)(2,1)S(1)}, u32[]{:S(2)}, u32[]{:S(2)}) collective-permute-start(bf16[8,5,128,128]{2,3,1,0:T(8,128)(2,1)S(1)} %get-tuple-element.21), channel_id=1, source_target_pairs={{0,16},{16,0},{4,20},{20,4},{8,24},{24,8},{12,28},{28,12},{32,48},... | collective-permute-start | bytes 3932168 | tf_op jit(solution)/shard_map/ppermute | solution.py:18
  125.9 4.1 %collective-permute-start.5 = (bf16[8,128,128]{2,1,0:T(8,128)(2,1)S(1)}, bf16[8,128,128]{2,1,0:T(8,128)(2,1)S(1)}, u32[]{:S(2)}, u32[]{:S(2)}) collective-permute-start(bf16[8,128,128]{2,1,0:T(8,128)(2,1)S(1)} %fusion.48), channel_id=1, source_target_pairs={{0,128},{128,0},{4,132},{132,4},{8,136},{136,8},{12,140},{140,12},... | collective-permute-start | bytes 786440 | tf_op jit(solution)/shard_map/ppermute | solution.py:18
  130.3 11.1 %collective-permute-done.5 = bf16[8,128,128]{2,1,0:T(8,128)(2,1)S(1)} collective-permute-done((bf16[8,128,128]{2,1,0:T(8,128)(2,1)S(1)}, bf16[8,128,128]{2,1,0:T(8,128)(2,1)S(1)}, u32[]{:S(2)}, u32[]{:S(2)}) %collective-permute-start.5) | collective-permute-done | bytes 262176 | tf_op jit(solution)/shard_map/ppermute | solution.py:18
  141.5 6.8 %collective-permute-start.6 = (bf16[8,128,128]{2,1,0:T(8,128)(2,1)S(1)}, bf16[8,128,128]{2,1,0:T(8,128)(2,1)S(1)}, u32[]{:S(2)}, u32[]{:S(2)}) collective-permute-start(bf16[8,128,128]{2,1,0:T(8,128)(2,1)S(1)} %fusion.29), channel_id=1, source_target_pairs={{0,256},{256,0},{4,260},{260,4},{8,264},{264,8},{12,268},{268,12},... | collective-permute-start | bytes 786440 | tf_op jit(solution)/shard_map/ppermute | solution.py:18
  148.5 33.7 %collective-permute-done.9 = bf16[8,5,128,128]{2,3,1,0:T(8,128)(2,1)S(1)} collective-permute-done((bf16[8,5,128,128]{2,3,1,0:T(8,128)(2,1)S(1)}, bf16[8,5,128,128]{2,3,1,0:T(8,128)(2,1)S(1)}, u32[]{:S(2)}, u32[]{:S(2)}) %collective-permute-start.9) | collective-permute-done | bytes 1310752 | tf_op jit(solution)/shard_map/ppermute | solution.py:18
  182.9 1.1 copy-done.4
  184.0 6.3 %collective-permute-start.10 = (bf16[8,4,128,128]{2,3,1,0:T(8,128)(2,1)S(1)}, bf16[8,4,128,128]{2,3,1,0:T(8,128)(2,1)S(1)}, u32[]{:S(2)}, u32[]{:S(2)}) collective-permute-start(bf16[8,4,128,128]{2,3,1,0:T(8,128)(2,1)S(1)} %get-tuple-element.19), channel_id=1, source_target_pairs={{0,32},{32,0},{4,36},{36,4},{8,40},{40,8},{12,44},{44,12},{16,48},... | collective-permute-start | bytes 3145736 | tf_op jit(solution)/shard_map/ppermute | solution.py:18
  191.8 1.0 multiply_reduce_fusion
  193.4 42.9 %collective-permute-done.10 = bf16[8,4,128,128]{2,3,1,0:T(8,128)(2,1)S(1)} collective-permute-done((bf16[8,4,128,128]{2,3,1,0:T(8,128)(2,1)S(1)}, bf16[8,4,128,128]{2,3,1,0:T(8,128)(2,1)S(1)}, u32[]{:S(2)}, u32[]{:S(2)}) %collective-permute-start.10) | collective-permute-done | bytes 1048608 | tf_op jit(solution)/shard_map/ppermute | solution.py:18
  236.5 1.8 fusion.108
  238.6 3.7 %collective-permute-start.11 = (bf16[8,3,128,128]{2,3,1,0:T(8,128)(2,1)}, bf16[8,3,128,128]{2,3,1,0:T(8,128)(2,1)}, u32[]{:S(2)}, u32[]{:S(2)}) collective-permute-start(bf16[8,3,128,128]{2,3,1,0:T(8,128)(2,1)} %get-tuple-element.17), channel_id=1, source_target_pairs={{0,64},{64,0},{4,68},{68,4},{8,72},{72,8},{12,76},{76,12},{16,80},... | collective-permute-start | bytes 2359304 | tf_op jit(solution)/shard_map/ppermute | solution.py:18
  242.5 1.3 fusion.115
  243.8 14.9 %collective-permute-done.11 = bf16[8,3,128,128]{2,3,1,0:T(8,128)(2,1)} collective-permute-done((bf16[8,3,128,128]{2,3,1,0:T(8,128)(2,1)}, bf16[8,3,128,128]{2,3,1,0:T(8,128)(2,1)}, u32[]{:S(2)}, u32[]{:S(2)}) %collective-permute-start.11) | collective-permute-done | bytes 786464 | tf_op jit(solution)/shard_map/ppermute | solution.py:18
  258.7 1.3 convert_element_type.203
  260.1 1.1 copy-done.7
  261.2 1.3 fusion.107
  262.5 3.0 collective-permute-start.12
  265.6 1.3 fusion.12
  267.0 2.3 fusion.74
  269.2 20.1 %collective-permute-done.12 = bf16[8,2,128,128]{2,3,1,0:T(8,128)(2,1)} collective-permute-done((bf16[8,2,128,128]{2,3,1,0:T(8,128)(2,1)}, bf16[8,2,128,128]{2,3,1,0:T(8,128)(2,1)}, u32[]{:S(2)}, u32[]{:S(2)}) %collective-permute-start.12) | collective-permute-done | bytes 524320 | tf_op jit(solution)/shard_map/ppermute | solution.py:18
  289.3 1.1 convert_element_type.205
  290.5 1.0 copy-done.11
  292.3 6.1 %collective-permute-start.13 = (bf16[8,1,128,128]{2,3,1,0:T(8,128)(2,1)}, bf16[8,1,128,128]{2,3,1,0:T(8,128)(2,1)}, u32[]{:S(2)}, u32[]{:S(2)}) collective-permute-start(bf16[8,1,128,128]{2,3,1,0:T(8,128)(2,1)} %fusion.30), channel_id=1, source_target_pairs={{0,256},{256,0},{4,260},{260,4},{8,264},{264,8},{12,268},{268,12},... | collective-permute-start | bytes 786440 | tf_op jit(solution)/shard_map/ppermute | solution.py:18
  300.4 1.8 copy.59
  302.2 1.8 copy.58
  304.0 1.6 convert_element_type.220
  305.6 5.6 %collective-permute-done.13 = bf16[8,1,128,128]{2,3,1,0:T(8,128)(2,1)} collective-permute-done((bf16[8,1,128,128]{2,3,1,0:T(8,128)(2,1)}, bf16[8,1,128,128]{2,3,1,0:T(8,128)(2,1)}, u32[]{:S(2)}, u32[]{:S(2)}) %collective-permute-start.13) | collective-permute-done | bytes 262176 | tf_op jit(solution)/shard_map/ppermute | solution.py:18
  311.2 2.1 fusion.34
  (120 shorter events, 12.8 us)
Async XLA Ops:
  7.2 35.9 %copy-start = (bf16[128,1024]{1,0:T(8,128)(2,1)S(1)}, bf16[128,1024]{1,0:T(8,128)(2,1)}, u32[]{:S(2)}) copy-start(bf16[128,1024]{1,0:T(8,128)(2,1)} %param.9) | copy-start | bytes 786436
  7.2 9.2 %copy-start.34 = (bf16[128,512]{1,0:T(8,128)(2,1)S(1)}, bf16[128,512]{1,0:T(8,128)(2,1)}, u32[]{:S(2)}) copy-start(bf16[128,512]{1,0:T(8,128)(2,1)} %param.10) | copy-start | bytes 393220
  9.1 19.4 %all-to-all-start = ((bf16[512,4,64]{0,2,1:T(8,128)(2,1)}), bf16[512,4,64]{0,2,1:T(8,128)(2,1)S(1)}, u32[]{:S(2)}, u32[]{:S(2)}) async-start(bf16[512,4,64]{0,2,1:T(8,128)(2,1)} %bitcast.3), calls=%async_computation | async-start | bytes 524288 | tf_op jit(solution)/shard_map/all_to_all | solution.py:30
  13.9 290.1 %reduce-scatter.2.cloned.1.call-start = ((), (), s32[]{:S(2)}) async-start(), calls=%async_computation.2 | async-start | bytes 1310720 | tf_op jit(solution)/shard_map/reduce_scatter | solution.py:139
  15.0 13.7 %copy-start.25 = (bf16[128,1024]{0,1:T(8,128)(2,1)}, bf16[128,1024]{0,1:T(8,128)(2,1)S(1)}, u32[]{:S(2)}) copy-start(bf16[128,1024]{0,1:T(8,128)(2,1)S(1)} %copy.47) | copy-start | bytes 786436
  15.0 13.7 %copy-start.35 = (s32[8]{0:T(128)S(1)}, s32[8]{0:T(128)}, u32[]{:S(2)}) copy-start(s32[8]{0:T(128)} %param.12) | copy-start | bytes 100
  16.1 44.0 %copy-start.12 = (bf16[16,8,8,128]{3,2,1,0:T(8,128)(2,1)}, bf16[16,8,8,128]{3,2,1,0:T(8,128)(2,1)S(1)}, u32[]{:S(2)}) copy-start(bf16[16,8,8,128]{3,2,1,0:T(8,128)(2,1)S(1)} %copy.101) | copy-start | bytes 786436
  16.2 14.1 %copy-start.8 = (f32[128,8,128]{0,2,1:T(8,128)}, f32[128,8,128]{0,2,1:T(8,128)S(1)}, u32[]{:S(2)}) copy-start(f32[128,8,128]{0,2,1:T(8,128)S(1)} %bitcast_convert_fusion) | copy-start | bytes 1572868
  28.4 5.1 %copy-start.28 = (bf16[4,8,8,512]{3,2,0,1:T(8,128)(2,1)}, bf16[4,8,8,512]{3,2,0,1:T(8,128)(2,1)S(1)}, u32[]{:S(2)}) copy-start(bf16[4,8,8,512]{3,2,0,1:T(8,128)(2,1)S(1)} %copy.100) | copy-start | bytes 786436
  30.3 3.2 copy-start.6
  30.3 12.5 %copy-start.19 = (bf16[128,1024]{1,0:T(8,128)(2,1)S(1)}, bf16[128,1024]{1,0:T(8,128)(2,1)}, u32[]{:S(2)}) copy-start(bf16[128,1024]{1,0:T(8,128)(2,1)} %param.8) | copy-start | bytes 786436
  33.5 16.0 %collective-permute-start.7 = (bf16[8,7,128,128]{2,3,1,0:T(8,128)(2,1)}, bf16[8,7,128,128]{2,3,1,0:T(8,128)(2,1)}, u32[]{:S(2)}, u32[]{:S(2)}) collective-permute-start(bf16[8,7,128,128]{2,3,1,0:T(8,128)(2,1)} %get-tuple-element.35), channel_id=1, source_target_pairs={{0,4},{4,0},{8,12},{12,8},{16,20},{20,16},{24,28},{28,24},{32,36},... | collective-permute-start | bytes 5505032 | tf_op jit(solution)/shard_map/ppermute | solution.py:18
  43.8 3.4 %collective-permute-start = (bf16[8,128,128]{2,1,0:T(8,128)(2,1)S(1)}, bf16[8,128,128]{2,1,0:T(8,128)(2,1)S(1)}, u32[]{:S(2)}, u32[]{:S(2)}) collective-permute-start(bf16[8,128,128]{2,1,0:T(8,128)(2,1)S(1)} %get-tuple-element.29), channel_id=1, source_target_pairs={{0,4},{4,0},{8,12},{12,8},{16,20},{20,16},{24,28},{28,24},{32,36},... | collective-permute-start | bytes 786440 | tf_op jit(solution)/shard_map/ppermute | solution.py:18
  47.3 4.2 %copy-start.2 = (f32[8,7,128,128]{2,3,1,0:T(8,128)S(1)}, f32[8,7,128,128]{2,3,1,0:T(8,128)}, u32[]{:S(2)}) copy-start(f32[8,7,128,128]{2,3,1,0:T(8,128)} %get-tuple-element.36) | copy-start | bytes 11010052
  47.3 10.8 %collective-permute-start.1 = (bf16[8,128,128]{2,1,0:T(8,128)(2,1)S(1)}, bf16[8,128,128]{2,1,0:T(8,128)(2,1)S(1)}, u32[]{:S(2)}, u32[]{:S(2)}) collective-permute-start(bf16[8,128,128]{2,1,0:T(8,128)(2,1)S(1)} %fusion.46), channel_id=1, source_target_pairs={{0,8},{8,0},{4,12},{12,4},{16,24},{24,16},{20,28},{28,20},{32,40},... | collective-permute-start | bytes 786440 | tf_op jit(solution)/shard_map/ppermute | solution.py:18
  51.5 3.3 %copy-start.1 = (f32[8,7,128,128]{2,3,1,0:T(8,128)}, f32[8,7,128,128]{2,3,1,0:T(8,128)S(1)}, u32[]{:S(2)}) copy-start(f32[8,7,128,128]{2,3,1,0:T(8,128)S(1)} %convert_element_type.195) | copy-start | bytes 11010052
  54.7 57.6 %collective-permute-start.8 = (bf16[8,6,128,128]{2,3,1,0:T(8,128)(2,1)}, bf16[8,6,128,128]{2,3,1,0:T(8,128)(2,1)}, u32[]{:S(2)}, u32[]{:S(2)}) collective-permute-start(bf16[8,6,128,128]{2,3,1,0:T(8,128)(2,1)} %get-tuple-element.23), channel_id=1, source_target_pairs={{0,8},{8,0},{4,12},{12,4},{16,24},{24,16},{20,28},{28,20},{32,40},... | collective-permute-start | bytes 4718600 | tf_op jit(solution)/shard_map/ppermute | solution.py:18
  58.2 39.0 %collective-permute-start.2 = (bf16[8,128,128]{2,1,0:T(8,128)(2,1)S(1)}, bf16[8,128,128]{2,1,0:T(8,128)(2,1)S(1)}, u32[]{:S(2)}, u32[]{:S(2)}) collective-permute-start(bf16[8,128,128]{2,1,0:T(8,128)(2,1)S(1)} %fusion.106), channel_id=1, source_target_pairs={{0,16},{16,0},{4,20},{20,4},{8,24},{24,8},{12,28},{28,12},{32,48},... | collective-permute-start | bytes 786440 | tf_op jit(solution)/shard_map/ppermute | solution.py:18
  60.4 49.5 %copy-start.21 = (bf16[128,8,128]{0,2,1:T(8,128)(2,1)}, bf16[128,8,128]{0,2,1:T(8,128)(2,1)S(1)}, u32[]{:S(2)}) copy-start(bf16[128,8,128]{0,2,1:T(8,128)(2,1)S(1)} %copy.51) | copy-start | bytes 786436
  60.8 131.0 %copy-start.30 = (bf16[8,128,128]{2,1,0:T(8,128)(2,1)}, bf16[8,128,128]{2,1,0:T(8,128)(2,1)S(1)}, u32[]{:S(2)}) copy-start(bf16[8,128,128]{2,1,0:T(8,128)(2,1)S(1)} %fusion.11) | copy-start | bytes 786436
  97.2 12.7 %copy-start.23 = (bf16[8,128,128]{2,1,0:T(8,128)(2,1)}, bf16[8,128,128]{2,1,0:T(8,128)(2,1)S(1)}, u32[]{:S(2)}) copy-start(bf16[8,128,128]{2,1,0:T(8,128)(2,1)S(1)} %collective-permute-done.2) | copy-start | bytes 786436
  97.4 12.4 %collective-permute-start.3 = (bf16[8,128,128]{2,1,0:T(8,128)(2,1)S(1)}, bf16[8,128,128]{2,1,0:T(8,128)(2,1)S(1)}, u32[]{:S(2)}, u32[]{:S(2)}) collective-permute-start(bf16[8,128,128]{2,1,0:T(8,128)(2,1)S(1)} %fusion.47), channel_id=1, source_target_pairs={{0,32},{32,0},{4,36},{36,4},{8,40},{40,8},{12,44},{44,12},{16,48},... | collective-permute-start | bytes 786440 | tf_op jit(solution)/shard_map/ppermute | solution.py:18
  110.0 4.2 %copy-start.3 = (f32[8,6,128,128]{2,3,1,0:T(8,128)S(1)}, f32[8,6,128,128]{2,3,1,0:T(8,128)}, u32[]{:S(2)}) copy-start(f32[8,6,128,128]{2,3,1,0:T(8,128)} %get-tuple-element.24) | copy-start | bytes 9437188
  110.0 15.9 %collective-permute-start.4 = (bf16[8,128,128]{2,1,0:T(8,128)(2,1)S(1)}, bf16[8,128,128]{2,1,0:T(8,128)(2,1)S(1)}, u32[]{:S(2)}, u32[]{:S(2)}) collective-permute-start(bf16[8,128,128]{2,1,0:T(8,128)(2,1)S(1)} %get-tuple-element.25), channel_id=1, source_target_pairs={{0,64},{64,0},{4,68},{68,4},{8,72},{72,8},{12,76},{76,12},{16,80},... | collective-permute-start | bytes 786440 | tf_op jit(solution)/shard_map/ppermute | solution.py:18
  114.1 11.6 %copy-start.24 = (bf16[8,128,128]{2,1,0:T(8,128)(2,1)S(1)}, bf16[8,128,128]{2,1,0:T(8,128)(2,1)}, u32[]{:S(2)}) copy-start(bf16[8,128,128]{2,1,0:T(8,128)(2,1)} %copy-done.23) | copy-start | bytes 786436
  114.7 67.5 %collective-permute-start.9 = (bf16[8,5,128,128]{2,3,1,0:T(8,128)(2,1)S(1)}, bf16[8,5,128,128]{2,3,1,0:T(8,128)(2,1)S(1)}, u32[]{:S(2)}, u32[]{:S(2)}) collective-permute-start(bf16[8,5,128,128]{2,3,1,0:T(8,128)(2,1)S(1)} %get-tuple-element.21), channel_id=1, source_target_pairs={{0,16},{16,0},{4,20},{20,4},{8,24},{24,8},{12,28},{28,12},{32,48},... | collective-permute-start | bytes 3932168 | tf_op jit(solution)/shard_map/ppermute | solution.py:18
  125.9 15.5 %collective-permute-start.5 = (bf16[8,128,128]{2,1,0:T(8,128)(2,1)S(1)}, bf16[8,128,128]{2,1,0:T(8,128)(2,1)S(1)}, u32[]{:S(2)}, u32[]{:S(2)}) collective-permute-start(bf16[8,128,128]{2,1,0:T(8,128)(2,1)S(1)} %fusion.48), channel_id=1, source_target_pairs={{0,128},{128,0},{4,132},{132,4},{8,136},{136,8},{12,140},{140,12},... | collective-permute-start | bytes 786440 | tf_op jit(solution)/shard_map/ppermute | solution.py:18
  141.5 48.8 %collective-permute-start.6 = (bf16[8,128,128]{2,1,0:T(8,128)(2,1)S(1)}, bf16[8,128,128]{2,1,0:T(8,128)(2,1)S(1)}, u32[]{:S(2)}, u32[]{:S(2)}) collective-permute-start(bf16[8,128,128]{2,1,0:T(8,128)(2,1)S(1)} %fusion.29), channel_id=1, source_target_pairs={{0,256},{256,0},{4,260},{260,4},{8,264},{264,8},{12,268},{268,12},... | collective-permute-start | bytes 786440 | tf_op jit(solution)/shard_map/ppermute | solution.py:18
  182.5 1.5 copy-start.4
  182.5 7.9 %copy-start.13 = (bf16[16,8,8,128]{3,2,1,0:T(8,128)(2,1)S(1)}, bf16[16,8,8,128]{3,2,1,0:T(8,128)(2,1)}, u32[]{:S(2)}) copy-start(bf16[16,8,8,128]{3,2,1,0:T(8,128)(2,1)} %copy-done.12) | copy-start | bytes 786436
  184.0 52.3 %collective-permute-start.10 = (bf16[8,4,128,128]{2,3,1,0:T(8,128)(2,1)S(1)}, bf16[8,4,128,128]{2,3,1,0:T(8,128)(2,1)S(1)}, u32[]{:S(2)}, u32[]{:S(2)}) collective-permute-start(bf16[8,4,128,128]{2,3,1,0:T(8,128)(2,1)S(1)} %get-tuple-element.19), channel_id=1, source_target_pairs={{0,32},{32,0},{4,36},{36,4},{8,40},{40,8},{12,44},{44,12},{16,48},... | collective-permute-start | bytes 3145736 | tf_op jit(solution)/shard_map/ppermute | solution.py:18
  190.4 1.3 copy-start.14
  190.5 1.3 copy-start.26
  190.5 2.3 copy-start.9
  236.5 2.1 copy-start.5
  236.5 5.9 %copy-start.29 = (bf16[4,8,8,512]{3,2,0,1:T(8,128)(2,1)S(1)}, bf16[4,8,8,512]{3,2,0,1:T(8,128)(2,1)}, u32[]{:S(2)}) copy-start(bf16[4,8,8,512]{3,2,0,1:T(8,128)(2,1)} %copy-done.28) | copy-start | bytes 786436
  238.6 20.1 %collective-permute-start.11 = (bf16[8,3,128,128]{2,3,1,0:T(8,128)(2,1)}, bf16[8,3,128,128]{2,3,1,0:T(8,128)(2,1)}, u32[]{:S(2)}, u32[]{:S(2)}) collective-permute-start(bf16[8,3,128,128]{2,3,1,0:T(8,128)(2,1)} %get-tuple-element.17), channel_id=1, source_target_pairs={{0,64},{64,0},{4,68},{68,4},{8,72},{72,8},{12,76},{76,12},{16,80},... | collective-permute-start | bytes 2359304 | tf_op jit(solution)/shard_map/ppermute | solution.py:18
  243.8 17.4 %copy-start.10 = (f32[8,3,128,128]{2,3,1,0:T(8,128)S(1)}, f32[8,3,128,128]{2,3,1,0:T(8,128)}, u32[]{:S(2)}) copy-start(f32[8,3,128,128]{2,3,1,0:T(8,128)} %get-tuple-element.18) | copy-start | bytes 4718596
  262.5 26.8 %collective-permute-start.12 = (bf16[8,2,128,128]{2,3,1,0:T(8,128)(2,1)}, bf16[8,2,128,128]{2,3,1,0:T(8,128)(2,1)}, u32[]{:S(2)}, u32[]{:S(2)}) collective-permute-start(bf16[8,2,128,128]{2,3,1,0:T(8,128)(2,1)} %get-tuple-element.15), channel_id=1, source_target_pairs={{0,128},{128,0},{4,132},{132,4},{8,136},{136,8},{12,140},{140,12},... | collective-permute-start | bytes 1572872 | tf_op jit(solution)/shard_map/ppermute | solution.py:18
  265.6 25.9 %copy-start.16 = (f32[8,2,128,128]{2,3,1,0:T(8,128)S(1)}, f32[8,2,128,128]{2,3,1,0:T(8,128)}, u32[]{:S(2)}) copy-start(f32[8,2,128,128]{2,3,1,0:T(8,128)} %get-tuple-element.16) | copy-start | bytes 3145732
  266.9 32.1 %copy-start.32 = (bf16[8,128,128]{2,1,0:T(8,128)(2,1)}, bf16[8,128,128]{2,1,0:T(8,128)(2,1)S(1)}, u32[]{:S(2)}) copy-start(bf16[8,128,128]{2,1,0:T(8,128)(2,1)S(1)} %fusion.12) | copy-start | bytes 786436
  266.9 31.5 %copy-start.15 = (bf16[8,7,128,128]{3,2,0,1:T(8,128)(2,1)S(1)}, bf16[8,7,128,128]{3,2,0,1:T(8,128)(2,1)}, u32[]{:S(2)}) copy-start(bf16[8,7,128,128]{3,2,0,1:T(8,128)(2,1)} %copy-done.14) | copy-start | bytes 5505028
  266.9 31.5 %copy-start.27 = (bf16[128,1024]{0,1:T(8,128)(2,1)S(1)}, bf16[128,1024]{0,1:T(8,128)(2,1)}, u32[]{:S(2)}) copy-start(bf16[128,1024]{0,1:T(8,128)(2,1)} %copy-done.25) | copy-start | bytes 786436
  292.3 18.9 %collective-permute-start.13 = (bf16[8,1,128,128]{2,3,1,0:T(8,128)(2,1)}, bf16[8,1,128,128]{2,3,1,0:T(8,128)(2,1)}, u32[]{:S(2)}, u32[]{:S(2)}) collective-permute-start(bf16[8,1,128,128]{2,3,1,0:T(8,128)(2,1)} %fusion.30), channel_id=1, source_target_pairs={{0,256},{256,0},{4,260},{260,4},{8,264},{264,8},{12,268},{268,12},... | collective-permute-start | bytes 786440 | tf_op jit(solution)/shard_map/ppermute | solution.py:18
  305.6 8.1 %copy-start.20 = (bf16[128,1024]{1,0:T(8,128)(2,1)S(1)}, bf16[128,1024]{1,0:T(8,128)(2,1)}, u32[]{:S(2)}) copy-start(bf16[128,1024]{1,0:T(8,128)(2,1)} %param.8) | copy-start | bytes 786436
  305.6 8.1 %copy-start.31 = (f32[8,128,128]{2,1,0:T(8,128)S(1)}, f32[8,128,128]{2,1,0:T(8,128)}, u32[]{:S(2)}) copy-start(f32[8,128,128]{2,1,0:T(8,128)} %fusion.74) | copy-start | bytes 1572868
  313.3 1.5 copy-start.22
  313.3 1.5 copy-start.33
  (4 other events, 3.8 us)
Sparse Core Ops, SparseCore 0:
  243.9 26.9 reduce-scatter.1
where the time goes:
time: 324 us; the launch traced here: 323 us
  waiting for transfers between devices  173 us (53%)
  starting transfers between devices  72.8 us (22%)
  other arithmetic  21.7 us (7%)
  between operations  15 us (5%)
  local copies, waits for them, and re-layouts  14.9 us (5%)
  matrix products  13.7 us (4%)
  blocking collectives  12 us (4%)
    ppermute x14, waiting for transfers between devices, from_partner(): return lax.ppermute(block, axis, route)  173 us
    ppermute x14, starting transfers between devices, from_partner(): return lax.ppermute(block, axis, route)  68 us
    unnamed x80, local copies, waits for them, and re-layouts  14.2 us
    all_gather x1, blocking collectives, local(): lax.all_gather(hidden, 'head', axis=1, tiled=True)  12 us
    convert_element_type x6, other arithmetic, local(): pending.astype(jnp.bfloat16)  8.11 us
    convert_element_type x6, other arithmetic, local(): from_partner(pending.astype(jnp.bfloat16), 'seq', bit_pos)  6.68 us
  transfers between devices with their start and end apart: 16, of which 9 were waited for; matrix products, arithmetic and copies ran while one was open for 10% of the time, Pallas kernels for 0%

commit v1 on v0

--- a/solution.py
+++ b/solution.py
@@ -30,7 +30,9 @@
     weight_cols = lax.all_to_all(gate_weight, "head", split_axis=1, concat_axis=0, tiled=True)
     logits = lax.dot_general(
         weight_cols,
-        lax.all_gather(hidden, "head", axis=1, tiled=True),
+        jnp.concatenate(
+            lax.all_to_all(jnp.stack([hidden] * lax.axis_size("head")), "head", 0, 0), axis=1
+        ),
         (((0,), (1,)), ((), ())),
         preferred_element_type=jnp.float32,
     )

time: 324 us -> 326 us (level)
  blocking collectives: 12 us -> 0 us
  starting transfers between devices: 72.8 us -> 79.3 us
  waiting for transfers between devices: 173 us -> 177 us
    all_gather x1 -> x0, blocking collectives: 12 us -> none  [local(): lax.all_gather(hidden, 'head', axis=1, tiled=True)]
    all_to_all x0 -> x1, waiting for transfers between devices: none -> 6.27 us  [local(): lax.all_to_all(jnp.stack([hidden] * lax.axis_size('head')), 'head', 0, 0)]
    ppermute x14, waiting for transfers between devices: 173 us -> 166 us  [from_partner(): return lax.ppermute(block, axis, route)]
    all_to_all x1, waiting for transfers between devices: 0.01 us -> 4.5 us  [local(): lax.all_to_all(gate_weight, 'head', split_axis=1, concat_axis=0, tiled=True)]
    all_to_all x0 -> x1, starting transfers between devices: none -> 3.47 us  [local(): lax.all_to_all(jnp.stack([hidden] * lax.axis_size('head')), 'head', 0, 0)]
    unnamed x80 -> x83, local copies, waits for them, and re-layouts: 14.2 us -> 13.3 us
  transfers between devices with their start and end apart: 16 -> 17, of which waited for: 9 -> 11; matrix products, arithmetic and copies ran while one was open for 10% -> 10% of each run, Pallas kernels for 0% -> 0%
where the time goes in v1:
time: 326 us; the launch traced here: 322 us
  waiting for transfers between devices  177 us (54%)
  starting transfers between devices  79.3 us (24%)
  other arithmetic  21.7 us (7%)
  between operations  15 us (5%)
  local copies, waits for them, and re-layouts  14.8 us (5%)
  matrix products  13.6 us (4%)
    ppermute x14, waiting for transfers between devices, from_partner(): return lax.ppermute(block, axis, route)  166 us
    ppermute x14, starting transfers between devices, from_partner(): return lax.ppermute(block, axis, route)  71 us
    unnamed x83, local copies, waits for them, and re-layouts  13.3 us
    convert_element_type x6, other arithmetic, local(): pending.astype(jnp.bfloat16)  8.1 us
    convert_element_type x6, other arithmetic, local(): from_partner(pending.astype(jnp.bfloat16), 'seq', bit_pos)  6.68 us
  transfers between devices with their start and end apart: 17, of which 11 were waited for; matrix products, arithmetic and copies ran while one was open for 10% of the time, Pallas kernels for 0%

profile of v1, /device:TPU:1, one launch (start us, length us, event | category | flops | bytes accessed | tf_op | source)
XLA Modules:
  0.0 321.7 jit_solution(4163312606137616097)
XLA Ops:
  7.2 1.9 copy.36
  9.1 4.8 %all-to-all-start = ((bf16[512,4,64]{0,2,1:T(8,128)(2,1)}), bf16[512,4,64]{0,2,1:T(8,128)(2,1)S(1)}, u32[]{:S(2)}, u32[]{:S(2)}) async-start(bf16[512,4,64]{0,2,1:T(8,128)(2,1)} %bitcast.3), calls=%async_computation | async-start | bytes 524288 | tf_op jit(solution)/shard_map/all_to_all | solution.py:30
  14.9 4.5 %all-to-all-done = bf16[512,4,64]{0,2,1:T(8,128)(2,1)S(1)} async-done(((bf16[512,4,64]{0,2,1:T(8,128)(2,1)}), bf16[512,4,64]{0,2,1:T(8,128)(2,1)S(1)}, u32[]{:S(2)}, u32[]{:S(2)}) %all-to-all-start) | async-done | bytes 262176 | tf_op jit(solution)/shard_map/all_to_all | solution.py:30
  20.3 3.5 %all-to-all-start.1 = ((bf16[4,128,512]{1,2,0:T(8,128)(2,1)}), bf16[4,128,512]{1,2,0:T(8,128)(2,1)S(1)}, u32[]{:S(2)}, u32[]{:S(2)}) async-start(bf16[4,128,512]{1,2,0:T(8,128)(2,1)} %stack.39), calls=%async_computation.1 | async-start | bytes 1048576 | tf_op jit(solution)/shard_map/all_to_all | solution.py:34
  24.4 6.3 %all-to-all-done.1 = bf16[4,128,512]{1,2,0:T(8,128)(2,1)S(1)} async-done(((bf16[4,128,512]{1,2,0:T(8,128)(2,1)}), bf16[4,128,512]{1,2,0:T(8,128)(2,1)S(1)}, u32[]{:S(2)}, u32[]{:S(2)}) %all-to-all-start.1) | async-done | bytes 524320 | tf_op jit(solution)/shard_map/all_to_all | solution.py:34
  31.1 1.3 multiply_convert_fusion
  32.5 3.2 %fusion.113 = (bf16[8,7,128,128]{2,3,1,0:T(8,128)(2,1)}, f32[8,7,128,128]{2,3,1,0:T(8,128)}) fusion(bf16[128,8,128,1]{2,1,0,3:T(8,128)(2,1)S(1)} %bitcast.212, bf16[128,8,8,128]{3,0,1,2:T(8,128)(2,1)S(1)} %multiply_convert_fusion), kind=kOutput, calls=%fused_computation.157 | convolution fusion | flops 235798528 | bytes 7602176 | tf_op jit(solution)/shard_map/thd,thje->hjde/dot_general | solution.py:61
  35.7 9.6 %collective-permute-start.7 = (bf16[8,7,128,128]{2,3,1,0:T(8,128)(2,1)}, bf16[8,7,128,128]{2,3,1,0:T(8,128)(2,1)}, u32[]{:S(2)}, u32[]{:S(2)}) collective-permute-start(bf16[8,7,128,128]{2,3,1,0:T(8,128)(2,1)} %get-tuple-element.35), channel_id=1, source_target_pairs={{0,4},{4,0},{8,12},{12,8},{16,20},{20,16},{24,28},{28,24},{32,36},... | collective-permute-start | bytes 5505032 | tf_op jit(solution)/shard_map/ppermute | solution.py:18
  46.3 1.9 collective-permute-start
  48.2 1.5 collective-permute-done
  49.8 2.2 collective-permute-start.1
  52.0 1.9 convert_element_type.195
  53.9 3.3 %fusion.110 = (bf16[8,6,128,128]{2,3,1,0:T(8,128)(2,1)}, f32[8,6,128,128]{2,3,1,0:T(8,128)}) fusion(f32[8,7,128,128]{2,3,1,0:T(8,128)S(1)} %convert_element_type.195, f32[8,7,128,128]{2,3,1,0:T(8,128)S(1)} %copy-done.2), kind=kLoop, calls=%fused_computation.154 | loop fusion | flops 1572864 | bytes 11010048 | tf_op jit(solution)/shard_map/convert_element_type | solution.py:83
  57.2 3.4 %collective-permute-start.8 = (bf16[8,6,128,128]{2,3,1,0:T(8,128)(2,1)}, bf16[8,6,128,128]{2,3,1,0:T(8,128)(2,1)}, u32[]{:S(2)}, u32[]{:S(2)}) collective-permute-start(bf16[8,6,128,128]{2,3,1,0:T(8,128)(2,1)} %get-tuple-element.23), channel_id=1, source_target_pairs={{0,8},{8,0},{4,12},{12,4},{16,24},{24,16},{20,28},{28,20},{32,40},... | collective-permute-start | bytes 4718600 | tf_op jit(solution)/shard_map/ppermute | solution.py:18
  60.7 2.3 collective-permute-start.2
  63.6 36.1 %collective-permute-done.2 = bf16[8,128,128]{2,1,0:T(8,128)(2,1)S(1)} collective-permute-done((bf16[8,128,128]{2,1,0:T(8,128)(2,1)S(1)}, bf16[8,128,128]{2,1,0:T(8,128)(2,1)S(1)}, u32[]{:S(2)}, u32[]{:S(2)}) %collective-permute-start.2) | collective-permute-done | bytes 262176 | tf_op jit(solution)/shard_map/ppermute | solution.py:18
  99.9 6.5 %collective-permute-start.3 = (bf16[8,128,128]{2,1,0:T(8,128)(2,1)S(1)}, bf16[8,128,128]{2,1,0:T(8,128)(2,1)S(1)}, u32[]{:S(2)}, u32[]{:S(2)}) collective-permute-start(bf16[8,128,128]{2,1,0:T(8,128)(2,1)S(1)} %fusion.45), channel_id=1, source_target_pairs={{0,32},{32,0},{4,36},{36,4},{8,40},{40,8},{12,44},{44,12},{16,48},... | collective-permute-start | bytes 786440 | tf_op jit(solution)/shard_map/ppermute | solution.py:18
  106.6 5.7 %collective-permute-done.3 = bf16[8,128,128]{2,1,0:T(8,128)(2,1)S(1)} collective-permute-done((bf16[8,128,128]{2,1,0:T(8,128)(2,1)S(1)}, bf16[8,128,128]{2,1,0:T(8,128)(2,1)S(1)}, u32[]{:S(2)}, u32[]{:S(2)}) %collective-permute-start.3) | collective-permute-done | bytes 262176 | tf_op jit(solution)/shard_map/ppermute | solution.py:18
  112.4 3.0 collective-permute-start.4
  115.4 1.8 convert_element_type.197
  117.7 11.0 %collective-permute-start.9 = (bf16[8,5,128,128]{2,3,1,0:T(8,128)(2,1)S(1)}, bf16[8,5,128,128]{2,3,1,0:T(8,128)(2,1)S(1)}, u32[]{:S(2)}, u32[]{:S(2)}) collective-permute-start(bf16[8,5,128,128]{2,3,1,0:T(8,128)(2,1)S(1)} %get-tuple-element.21), channel_id=1, source_target_pairs={{0,16},{16,0},{4,20},{20,4},{8,24},{24,8},{12,28},{28,12},{32,48},... | collective-permute-start | bytes 3932168 | tf_op jit(solution)/shard_map/ppermute | solution.py:18
  128.9 4.2 %collective-permute-start.5 = (bf16[8,128,128]{2,1,0:T(8,128)(2,1)S(1)}, bf16[8,128,128]{2,1,0:T(8,128)(2,1)S(1)}, u32[]{:S(2)}, u32[]{:S(2)}) collective-permute-start(bf16[8,128,128]{2,1,0:T(8,128)(2,1)S(1)} %fusion.46), channel_id=1, source_target_pairs={{0,128},{128,0},{4,132},{132,4},{8,136},{136,8},{12,140},{140,12},... | collective-permute-start | bytes 786440 | tf_op jit(solution)/shard_map/ppermute | solution.py:18
  133.3 11.5 %collective-permute-done.5 = bf16[8,128,128]{2,1,0:T(8,128)(2,1)S(1)} collective-permute-done((bf16[8,128,128]{2,1,0:T(8,128)(2,1)S(1)}, bf16[8,128,128]{2,1,0:T(8,128)(2,1)S(1)}, u32[]{:S(2)}, u32[]{:S(2)}) %collective-permute-start.5) | collective-permute-done | bytes 262176 | tf_op jit(solution)/shard_map/ppermute | solution.py:18
  144.9 6.4 %collective-permute-start.6 = (bf16[8,128,128]{2,1,0:T(8,128)(2,1)S(1)}, bf16[8,128,128]{2,1,0:T(8,128)(2,1)S(1)}, u32[]{:S(2)}, u32[]{:S(2)}) collective-permute-start(bf16[8,128,128]{2,1,0:T(8,128)(2,1)S(1)} %fusion.29), channel_id=1, source_target_pairs={{0,256},{256,0},{4,260},{260,4},{8,264},{264,8},{12,268},{268,12},... | collective-permute-start | bytes 786440 | tf_op jit(solution)/shard_map/ppermute | solution.py:18
  151.5 33.5 %collective-permute-done.9 = bf16[8,5,128,128]{2,3,1,0:T(8,128)(2,1)S(1)} collective-permute-done((bf16[8,5,128,128]{2,3,1,0:T(8,128)(2,1)S(1)}, bf16[8,5,128,128]{2,3,1,0:T(8,128)(2,1)S(1)}, u32[]{:S(2)}, u32[]{:S(2)}) %collective-permute-start.9) | collective-permute-done | bytes 1310752 | tf_op jit(solution)/shard_map/ppermute | solution.py:18
  185.8 1.1 copy-done.4
  186.9 6.5 %collective-permute-start.10 = (bf16[8,4,128,128]{2,3,1,0:T(8,128)(2,1)S(1)}, bf16[8,4,128,128]{2,3,1,0:T(8,128)(2,1)S(1)}, u32[]{:S(2)}, u32[]{:S(2)}) collective-permute-start(bf16[8,4,128,128]{2,3,1,0:T(8,128)(2,1)S(1)} %get-tuple-element.19), channel_id=1, source_target_pairs={{0,32},{32,0},{4,36},{36,4},{8,40},{40,8},{12,44},{44,12},{16,48},... | collective-permute-start | bytes 3145736 | tf_op jit(solution)/shard_map/ppermute | solution.py:18
  194.8 1.0 multiply_reduce_fusion
  196.4 42.6 %collective-permute-done.10 = bf16[8,4,128,128]{2,3,1,0:T(8,128)(2,1)S(1)} collective-permute-done((bf16[8,4,128,128]{2,3,1,0:T(8,128)(2,1)S(1)}, bf16[8,4,128,128]{2,3,1,0:T(8,128)(2,1)S(1)}, u32[]{:S(2)}, u32[]{:S(2)}) %collective-permute-start.10) | collective-permute-done | bytes 1048608 | tf_op jit(solution)/shard_map/ppermute | solution.py:18
  239.2 1.8 fusion.107
  241.3 3.1 collective-permute-start.11
  244.6 1.3 fusion.114
  245.9 14.7 %collective-permute-done.11 = bf16[8,3,128,128]{2,3,1,0:T(8,128)(2,1)} collective-permute-done((bf16[8,3,128,128]{2,3,1,0:T(8,128)(2,1)}, bf16[8,3,128,128]{2,3,1,0:T(8,128)(2,1)}, u32[]{:S(2)}, u32[]{:S(2)}) %collective-permute-start.11) | collective-permute-done | bytes 786464 | tf_op jit(solution)/shard_map/ppermute | solution.py:18
  260.6 1.3 convert_element_type.203
  261.9 1.1 copy-done.7
  263.0 1.3 fusion.106
  264.4 4.2 %collective-permute-start.12 = (bf16[8,2,128,128]{2,3,1,0:T(8,128)(2,1)}, bf16[8,2,128,128]{2,3,1,0:T(8,128)(2,1)}, u32[]{:S(2)}, u32[]{:S(2)}) collective-permute-start(bf16[8,2,128,128]{2,3,1,0:T(8,128)(2,1)} %get-tuple-element.15), channel_id=1, source_target_pairs={{0,128},{128,0},{4,132},{132,4},{8,136},{136,8},{12,140},{140,12},... | collective-permute-start | bytes 1572872 | tf_op jit(solution)/shard_map/ppermute | solution.py:18
  268.6 1.3 fusion.12
  270.0 2.3 fusion.73
  272.3 19.2 %collective-permute-done.12 = bf16[8,2,128,128]{2,3,1,0:T(8,128)(2,1)} collective-permute-done((bf16[8,2,128,128]{2,3,1,0:T(8,128)(2,1)}, bf16[8,2,128,128]{2,3,1,0:T(8,128)(2,1)}, u32[]{:S(2)}, u32[]{:S(2)}) %collective-permute-start.12) | collective-permute-done | bytes 524320 | tf_op jit(solution)/shard_map/ppermute | solution.py:18
  291.5 1.1 convert_element_type.205
  292.6 1.0 copy-done.11
  294.4 6.8 %collective-permute-start.13 = (bf16[8,1,128,128]{2,3,1,0:T(8,128)(2,1)}, bf16[8,1,128,128]{2,3,1,0:T(8,128)(2,1)}, u32[]{:S(2)}, u32[]{:S(2)}) collective-permute-start(bf16[8,1,128,128]{2,3,1,0:T(8,128)(2,1)} %fusion.30), channel_id=1, source_target_pairs={{0,256},{256,0},{4,260},{260,4},{8,264},{264,8},{12,268},{268,12},... | collective-permute-start | bytes 786440 | tf_op jit(solution)/shard_map/ppermute | solution.py:18
  303.2 1.8 copy.60
  305.0 1.8 copy.59
  306.8 1.6 convert_element_type.220
  308.4 1.7 collective-permute-done.13
  310.1 2.1 fusion.34
  (125 shorter events, 14.8 us)
Async XLA Ops:
  7.2 38.4 %copy-start = (bf16[128,1024]{1,0:T(8,128)(2,1)S(1)}, bf16[128,1024]{1,0:T(8,128)(2,1)}, u32[]{:S(2)}) copy-start(bf16[128,1024]{1,0:T(8,128)(2,1)} %param.9) | copy-start | bytes 786436
  7.2 16.7 %copy-start.34 = (bf16[128,1024]{1,0:T(8,128)(2,1)S(1)}, bf16[128,1024]{1,0:T(8,128)(2,1)}, u32[]{:S(2)}) copy-start(bf16[128,1024]{1,0:T(8,128)(2,1)} %param.13) | copy-start | bytes 786436
  7.2 16.8 %copy-start.35 = (bf16[128,1024]{1,0:T(8,128)(2,1)S(1)}, bf16[128,1024]{1,0:T(8,128)(2,1)}, u32[]{:S(2)}) copy-start(bf16[128,1024]{1,0:T(8,128)(2,1)} %param.7) | copy-start | bytes 786436
  9.1 10.4 %all-to-all-start = ((bf16[512,4,64]{0,2,1:T(8,128)(2,1)}), bf16[512,4,64]{0,2,1:T(8,128)(2,1)S(1)}, u32[]{:S(2)}, u32[]{:S(2)}) async-start(bf16[512,4,64]{0,2,1:T(8,128)(2,1)} %bitcast.3), calls=%async_computation | async-start | bytes 524288 | tf_op jit(solution)/shard_map/all_to_all | solution.py:30
  20.3 10.4 %all-to-all-start.1 = ((bf16[4,128,512]{1,2,0:T(8,128)(2,1)}), bf16[4,128,512]{1,2,0:T(8,128)(2,1)S(1)}, u32[]{:S(2)}, u32[]{:S(2)}) async-start(bf16[4,128,512]{1,2,0:T(8,128)(2,1)} %stack.39), calls=%async_computation.1 | async-start | bytes 1048576 | tf_op jit(solution)/shard_map/all_to_all | solution.py:34
  23.8 7.1 %copy-start.36 = (s32[8]{0:T(128)S(1)}, s32[8]{0:T(128)}, u32[]{:S(2)}) copy-start(s32[8]{0:T(128)} %param.12) | copy-start | bytes 100
  23.8 283.0 %reduce-scatter.2.cloned.1.call-start = ((), (), s32[]{:S(2)}) async-start(), calls=%async_computation.3 | async-start | bytes 1310720 | tf_op jit(solution)/shard_map/reduce_scatter | solution.py:141
  24.0 8.4 %copy-start.25 = (bf16[128,1024]{0,1:T(8,128)(2,1)}, bf16[128,1024]{0,1:T(8,128)(2,1)S(1)}, u32[]{:S(2)}) copy-start(bf16[128,1024]{0,1:T(8,128)(2,1)S(1)} %copy.48) | copy-start | bytes 786436
  24.1 38.9 %copy-start.12 = (bf16[16,8,8,128]{3,2,1,0:T(8,128)(2,1)}, bf16[16,8,8,128]{3,2,1,0:T(8,128)(2,1)S(1)}, u32[]{:S(2)}) copy-start(bf16[16,8,8,128]{3,2,1,0:T(8,128)(2,1)S(1)} %copy.102) | copy-start | bytes 786436
  24.1 8.3 %copy-start.8 = (f32[128,8,128]{0,2,1:T(8,128)}, f32[128,8,128]{0,2,1:T(8,128)S(1)}, u32[]{:S(2)}) copy-start(f32[128,8,128]{0,2,1:T(8,128)S(1)} %bitcast_convert_fusion) | copy-start | bytes 1572868
  24.4 11.3 %copy-start.28 = (bf16[4,8,8,512]{3,2,0,1:T(8,128)(2,1)}, bf16[4,8,8,512]{3,2,0,1:T(8,128)(2,1)S(1)}, u32[]{:S(2)}) copy-start(bf16[4,8,8,512]{3,2,0,1:T(8,128)(2,1)S(1)} %copy.101) | copy-start | bytes 786436
  32.4 3.2 %copy-start.6 = (bf16[128,8,8,128]{3,0,1,2:T(8,128)(2,1)}, bf16[128,8,8,128]{3,0,1,2:T(8,128)(2,1)S(1)}, u32[]{:S(2)}) copy-start(bf16[128,8,8,128]{3,0,1,2:T(8,128)(2,1)S(1)} %multiply_convert_fusion) | copy-start | bytes 6291460
  32.4 12.8 %copy-start.19 = (bf16[128,1024]{1,0:T(8,128)(2,1)S(1)}, bf16[128,1024]{1,0:T(8,128)(2,1)}, u32[]{:S(2)}) copy-start(bf16[128,1024]{1,0:T(8,128)(2,1)} %param.8) | copy-start | bytes 786436
  35.7 16.3 %collective-permute-start.7 = (bf16[8,7,128,128]{2,3,1,0:T(8,128)(2,1)}, bf16[8,7,128,128]{2,3,1,0:T(8,128)(2,1)}, u32[]{:S(2)}, u32[]{:S(2)}) collective-permute-start(bf16[8,7,128,128]{2,3,1,0:T(8,128)(2,1)} %get-tuple-element.35), channel_id=1, source_target_pairs={{0,4},{4,0},{8,12},{12,8},{16,20},{20,16},{24,28},{28,24},{32,36},... | collective-permute-start | bytes 5505032 | tf_op jit(solution)/shard_map/ppermute | solution.py:18
  46.3 3.4 %collective-permute-start = (bf16[8,128,128]{2,1,0:T(8,128)(2,1)S(1)}, bf16[8,128,128]{2,1,0:T(8,128)(2,1)S(1)}, u32[]{:S(2)}, u32[]{:S(2)}) collective-permute-start(bf16[8,128,128]{2,1,0:T(8,128)(2,1)S(1)} %get-tuple-element.29), channel_id=1, source_target_pairs={{0,4},{4,0},{8,12},{12,8},{16,20},{20,16},{24,28},{28,24},{32,36},... | collective-permute-start | bytes 786440 | tf_op jit(solution)/shard_map/ppermute | solution.py:18
  49.8 4.2 %copy-start.2 = (f32[8,7,128,128]{2,3,1,0:T(8,128)S(1)}, f32[8,7,128,128]{2,3,1,0:T(8,128)}, u32[]{:S(2)}) copy-start(f32[8,7,128,128]{2,3,1,0:T(8,128)} %get-tuple-element.36) | copy-start | bytes 11010052
  49.8 10.8 %collective-permute-start.1 = (bf16[8,128,128]{2,1,0:T(8,128)(2,1)S(1)}, bf16[8,128,128]{2,1,0:T(8,128)(2,1)S(1)}, u32[]{:S(2)}, u32[]{:S(2)}) collective-permute-start(bf16[8,128,128]{2,1,0:T(8,128)(2,1)S(1)} %fusion.44), channel_id=1, source_target_pairs={{0,8},{8,0},{4,12},{12,4},{16,24},{24,16},{20,28},{28,20},{32,40},... | collective-permute-start | bytes 786440 | tf_op jit(solution)/shard_map/ppermute | solution.py:18
  53.9 3.3 %copy-start.1 = (f32[8,7,128,128]{2,3,1,0:T(8,128)}, f32[8,7,128,128]{2,3,1,0:T(8,128)S(1)}, u32[]{:S(2)}) copy-start(f32[8,7,128,128]{2,3,1,0:T(8,128)S(1)} %convert_element_type.195) | copy-start | bytes 11010052
  57.2 58.2 %collective-permute-start.8 = (bf16[8,6,128,128]{2,3,1,0:T(8,128)(2,1)}, bf16[8,6,128,128]{2,3,1,0:T(8,128)(2,1)}, u32[]{:S(2)}, u32[]{:S(2)}) collective-permute-start(bf16[8,6,128,128]{2,3,1,0:T(8,128)(2,1)} %get-tuple-element.23), channel_id=1, source_target_pairs={{0,8},{8,0},{4,12},{12,4},{16,24},{24,16},{20,28},{28,20},{32,40},... | collective-permute-start | bytes 4718600 | tf_op jit(solution)/shard_map/ppermute | solution.py:18
  60.7 39.0 %collective-permute-start.2 = (bf16[8,128,128]{2,1,0:T(8,128)(2,1)S(1)}, bf16[8,128,128]{2,1,0:T(8,128)(2,1)S(1)}, u32[]{:S(2)}, u32[]{:S(2)}) collective-permute-start(bf16[8,128,128]{2,1,0:T(8,128)(2,1)S(1)} %fusion.105), channel_id=1, source_target_pairs={{0,16},{16,0},{4,20},{20,4},{8,24},{24,8},{12,28},{28,12},{32,48},... | collective-permute-start | bytes 786440 | tf_op jit(solution)/shard_map/ppermute | solution.py:18
  63.3 49.2 %copy-start.21 = (bf16[128,8,128]{0,2,1:T(8,128)(2,1)}, bf16[128,8,128]{0,2,1:T(8,128)(2,1)S(1)}, u32[]{:S(2)}) copy-start(bf16[128,8,128]{0,2,1:T(8,128)(2,1)S(1)} %copy.52) | copy-start | bytes 786436
  63.6 131.2 %copy-start.30 = (bf16[8,128,128]{2,1,0:T(8,128)(2,1)}, bf16[8,128,128]{2,1,0:T(8,128)(2,1)S(1)}, u32[]{:S(2)}) copy-start(bf16[8,128,128]{2,1,0:T(8,128)(2,1)S(1)} %fusion.11) | copy-start | bytes 786436
  99.7 12.7 %copy-start.23 = (bf16[8,128,128]{2,1,0:T(8,128)(2,1)}, bf16[8,128,128]{2,1,0:T(8,128)(2,1)S(1)}, u32[]{:S(2)}) copy-start(bf16[8,128,128]{2,1,0:T(8,128)(2,1)S(1)} %collective-permute-done.2) | copy-start | bytes 786436
  99.9 12.4 %collective-permute-start.3 = (bf16[8,128,128]{2,1,0:T(8,128)(2,1)S(1)}, bf16[8,128,128]{2,1,0:T(8,128)(2,1)S(1)}, u32[]{:S(2)}, u32[]{:S(2)}) collective-permute-start(bf16[8,128,128]{2,1,0:T(8,128)(2,1)S(1)} %fusion.45), channel_id=1, source_target_pairs={{0,32},{32,0},{4,36},{36,4},{8,40},{40,8},{12,44},{44,12},{16,48},... | collective-permute-start | bytes 786440 | tf_op jit(solution)/shard_map/ppermute | solution.py:18
  112.4 4.8 %copy-start.3 = (f32[8,6,128,128]{2,3,1,0:T(8,128)S(1)}, f32[8,6,128,128]{2,3,1,0:T(8,128)}, u32[]{:S(2)}) copy-start(f32[8,6,128,128]{2,3,1,0:T(8,128)} %get-tuple-element.24) | copy-start | bytes 9437188
  112.4 16.4 %collective-permute-start.4 = (bf16[8,128,128]{2,1,0:T(8,128)(2,1)S(1)}, bf16[8,128,128]{2,1,0:T(8,128)(2,1)S(1)}, u32[]{:S(2)}, u32[]{:S(2)}) collective-permute-start(bf16[8,128,128]{2,1,0:T(8,128)(2,1)S(1)} %get-tuple-element.25), channel_id=1, source_target_pairs={{0,64},{64,0},{4,68},{68,4},{8,72},{72,8},{12,76},{76,12},{16,80},... | collective-permute-start | bytes 786440 | tf_op jit(solution)/shard_map/ppermute | solution.py:18
  117.2 11.5 %copy-start.24 = (bf16[8,128,128]{2,1,0:T(8,128)(2,1)S(1)}, bf16[8,128,128]{2,1,0:T(8,128)(2,1)}, u32[]{:S(2)}) copy-start(bf16[8,128,128]{2,1,0:T(8,128)(2,1)} %copy-done.23) | copy-start | bytes 786436
  117.7 67.3 %collective-permute-start.9 = (bf16[8,5,128,128]{2,3,1,0:T(8,128)(2,1)S(1)}, bf16[8,5,128,128]{2,3,1,0:T(8,128)(2,1)S(1)}, u32[]{:S(2)}, u32[]{:S(2)}) collective-permute-start(bf16[8,5,128,128]{2,3,1,0:T(8,128)(2,1)S(1)} %get-tuple-element.21), channel_id=1, source_target_pairs={{0,16},{16,0},{4,20},{20,4},{8,24},{24,8},{12,28},{28,12},{32,48},... | collective-permute-start | bytes 3932168 | tf_op jit(solution)/shard_map/ppermute | solution.py:18
  128.9 16.0 %collective-permute-start.5 = (bf16[8,128,128]{2,1,0:T(8,128)(2,1)S(1)}, bf16[8,128,128]{2,1,0:T(8,128)(2,1)S(1)}, u32[]{:S(2)}, u32[]{:S(2)}) collective-permute-start(bf16[8,128,128]{2,1,0:T(8,128)(2,1)S(1)} %fusion.46), channel_id=1, source_target_pairs={{0,128},{128,0},{4,132},{132,4},{8,136},{136,8},{12,140},{140,12},... | collective-permute-start | bytes 786440 | tf_op jit(solution)/shard_map/ppermute | solution.py:18
  144.9 48.4 %collective-permute-start.6 = (bf16[8,128,128]{2,1,0:T(8,128)(2,1)S(1)}, bf16[8,128,128]{2,1,0:T(8,128)(2,1)S(1)}, u32[]{:S(2)}, u32[]{:S(2)}) collective-permute-start(bf16[8,128,128]{2,1,0:T(8,128)(2,1)S(1)} %fusion.29), channel_id=1, source_target_pairs={{0,256},{256,0},{4,260},{260,4},{8,264},{264,8},{12,268},{268,12},... | collective-permute-start | bytes 786440 | tf_op jit(solution)/shard_map/ppermute | solution.py:18
  185.3 1.5 copy-start.4
  185.4 8.1 %copy-start.13 = (bf16[16,8,8,128]{3,2,1,0:T(8,128)(2,1)S(1)}, bf16[16,8,8,128]{3,2,1,0:T(8,128)(2,1)}, u32[]{:S(2)}) copy-start(bf16[16,8,8,128]{3,2,1,0:T(8,128)(2,1)} %copy-done.12) | copy-start | bytes 786436
  186.9 52.1 %collective-permute-start.10 = (bf16[8,4,128,128]{2,3,1,0:T(8,128)(2,1)S(1)}, bf16[8,4,128,128]{2,3,1,0:T(8,128)(2,1)S(1)}, u32[]{:S(2)}, u32[]{:S(2)}) collective-permute-start(bf16[8,4,128,128]{2,3,1,0:T(8,128)(2,1)S(1)} %get-tuple-element.19), channel_id=1, source_target_pairs={{0,32},{32,0},{4,36},{36,4},{8,40},{40,8},{12,44},{44,12},{16,48},... | collective-permute-start | bytes 3145736 | tf_op jit(solution)/shard_map/ppermute | solution.py:18
  193.5 2.3 copy-start.9
  239.2 2.1 copy-start.5
  239.2 5.4 %copy-start.29 = (bf16[4,8,8,512]{3,2,0,1:T(8,128)(2,1)S(1)}, bf16[4,8,8,512]{3,2,0,1:T(8,128)(2,1)}, u32[]{:S(2)}) copy-start(bf16[4,8,8,512]{3,2,0,1:T(8,128)(2,1)} %copy-done.28) | copy-start | bytes 786436
  241.3 19.3 %collective-permute-start.11 = (bf16[8,3,128,128]{2,3,1,0:T(8,128)(2,1)}, bf16[8,3,128,128]{2,3,1,0:T(8,128)(2,1)}, u32[]{:S(2)}, u32[]{:S(2)}) collective-permute-start(bf16[8,3,128,128]{2,3,1,0:T(8,128)(2,1)} %get-tuple-element.17), channel_id=1, source_target_pairs={{0,64},{64,0},{4,68},{68,4},{8,72},{72,8},{12,76},{76,12},{16,80},... | collective-permute-start | bytes 2359304 | tf_op jit(solution)/shard_map/ppermute | solution.py:18
  245.9 17.1 %copy-start.10 = (f32[8,3,128,128]{2,3,1,0:T(8,128)S(1)}, f32[8,3,128,128]{2,3,1,0:T(8,128)}, u32[]{:S(2)}) copy-start(f32[8,3,128,128]{2,3,1,0:T(8,128)} %get-tuple-element.18) | copy-start | bytes 4718596
  264.4 27.1 %collective-permute-start.12 = (bf16[8,2,128,128]{2,3,1,0:T(8,128)(2,1)}, bf16[8,2,128,128]{2,3,1,0:T(8,128)(2,1)}, u32[]{:S(2)}, u32[]{:S(2)}) collective-permute-start(bf16[8,2,128,128]{2,3,1,0:T(8,128)(2,1)} %get-tuple-element.15), channel_id=1, source_target_pairs={{0,128},{128,0},{4,132},{132,4},{8,136},{136,8},{12,140},{140,12},... | collective-permute-start | bytes 1572872 | tf_op jit(solution)/shard_map/ppermute | solution.py:18
  268.6 25.0 %copy-start.16 = (f32[8,2,128,128]{2,3,1,0:T(8,128)S(1)}, f32[8,2,128,128]{2,3,1,0:T(8,128)}, u32[]{:S(2)}) copy-start(f32[8,2,128,128]{2,3,1,0:T(8,128)} %get-tuple-element.16) | copy-start | bytes 3145732
  270.0 32.0 %copy-start.32 = (bf16[8,128,128]{2,1,0:T(8,128)(2,1)}, bf16[8,128,128]{2,1,0:T(8,128)(2,1)S(1)}, u32[]{:S(2)}) copy-start(bf16[8,128,128]{2,1,0:T(8,128)(2,1)S(1)} %fusion.12) | copy-start | bytes 786436
  270.0 31.3 %copy-start.15 = (bf16[8,7,128,128]{3,2,0,1:T(8,128)(2,1)S(1)}, bf16[8,7,128,128]{3,2,0,1:T(8,128)(2,1)}, u32[]{:S(2)}) copy-start(bf16[8,7,128,128]{3,2,0,1:T(8,128)(2,1)} %copy-done.14) | copy-start | bytes 5505028
  270.0 31.3 %copy-start.27 = (bf16[128,1024]{0,1:T(8,128)(2,1)S(1)}, bf16[128,1024]{0,1:T(8,128)(2,1)}, u32[]{:S(2)}) copy-start(bf16[128,1024]{0,1:T(8,128)(2,1)} %copy-done.25) | copy-start | bytes 786436
  294.4 15.7 %collective-permute-start.13 = (bf16[8,1,128,128]{2,3,1,0:T(8,128)(2,1)}, bf16[8,1,128,128]{2,3,1,0:T(8,128)(2,1)}, u32[]{:S(2)}, u32[]{:S(2)}) collective-permute-start(bf16[8,1,128,128]{2,3,1,0:T(8,128)(2,1)} %fusion.30), channel_id=1, source_target_pairs={{0,256},{256,0},{4,260},{260,4},{8,264},{264,8},{12,268},{268,12},... | collective-permute-start | bytes 786440 | tf_op jit(solution)/shard_map/ppermute | solution.py:18
  308.4 4.2 %copy-start.20 = (bf16[128,1024]{1,0:T(8,128)(2,1)S(1)}, bf16[128,1024]{1,0:T(8,128)(2,1)}, u32[]{:S(2)}) copy-start(bf16[128,1024]{1,0:T(8,128)(2,1)} %param.8) | copy-start | bytes 786436
  308.4 4.2 %copy-start.31 = (f32[8,128,128]{2,1,0:T(8,128)S(1)}, f32[8,128,128]{2,1,0:T(8,128)}, u32[]{:S(2)}) copy-start(f32[8,128,128]{2,1,0:T(8,128)} %fusion.73) | copy-start | bytes 1572868
  312.3 1.5 copy-start.22
  312.3 1.5 copy-start.33
  (6 other events, 6.4 us)
Sparse Core Ops, SparseCore 0:
  246.0 26.0 reduce-scatter.1
